TPU v7x, 32 devices: a whole 2x2x4 slice. The times are simulated.
32 devices in a mesh: frame: 4 (over x, core), tile: 8 (over z, y).
Axes of the slice: x: 2, y: 2, z: 4, core: 2. Of those that a mesh axis runs over, the one named last changes fastest.
Arguments:
- frames: bfloat16 [4, 64, 64, 2048], P('frame', None, 'tile'), may hold values from -6 to 6
- predict_w: bfloat16 [2, 4, 3, 3, 64, 64], replicated, may hold values from -0.25 to 0.25
- predict_b: float32 [2, 4, 64], replicated, may hold values from -2 to 2
- update_w: bfloat16 [2, 4, 3, 3, 64, 64], replicated, may hold values from -0.25 to 0.25
- update_b: float32 [2, 4, 64], replicated, may hold values from -2 to 2
Outputs:
- coefficients: bfloat16 [4, 64, 64, 2048], P('frame', None, 'tile')
All inputs are finite; a program needn't handle non-finite values.
Results may differ from a plain program's by a relative error of at most 0.009.
Values may be sent and summed in bfloat16 or wider, within the bound.
A program may use at most 128 MiB of HBM per device.

v0:
```python
import functools

import jax
import jax.numpy as jnp
from jax import lax
from jax.experimental import pallas as pl
from jax.experimental.pallas import tpu as pltpu
from jax.sharding import PartitionSpec as P

LANES = 128
MESSAGES = (
    "down0", "down1", "up0", "up1", "even0", "even1", "odd",
    "hs0", "hs1", "hh0", "hh1", "x", "x2", "x3", "fs", "fh", "gs", "gh", "hl", "l1", "l2", "l3",
)
SLOT = {name: k for k, name in enumerate(MESSAGES)}
LOCAL = ("own", "base", "keep", "out", "out2")
LSLOT = {name: k for k, name in enumerate(LOCAL)}


def build_weights(k_ref, level, w_ref):
    layers, channels = k_ref.shape[1], k_ref.shape[5]
    w_ref[...] = jnp.zeros_like(w_ref)
    for layer in range(layers):
        for s in range(3):
            for p in range(2):
                top = (2 * s + p) * channels
                for r in range(3):
                    q = r + p
                    w_ref[layer, top : top + channels, q * channels : (q + 1) * channels] = k_ref[
                        level, layer, r, s
                    ]


def kernel(tiles, own, pw, uw, pb, ub, out, e, h, b1, low, f2, h2, o2, l2, wa, wb, wc, wd, a_ref, c_ref, d_ref, send_sem, recv_sem, local_sem):
    own_rows, channels, width = own.shape
    half = own_rows // 2
    layers = pw.shape[1]
    part = width // 2
    block = part + LANES
    f = lax.axis_index("frame")
    t = lax.axis_index("tile")
    core = lax.rem(f, 2)
    upper = lax.rem(lax.div(f, 2), 2)
    partner = f + 1 - 2 * core
    across = f + 2 - 4 * upper
    diagonal = across + 1 - 2 * core
    has_up, has_down = t > 0, t < tiles - 1
    is_even, is_odd = core == 0, core == 1
    is_lower, is_upper = upper == 0, upper == 1
    first_row = t * own_rows + core * half - layers
    halo_tile = t + 2 * core - 1
    has_halo = jnp.logical_and(halo_tile >= 0, halo_tile < tiles)

    barrier = pltpu.get_barrier_semaphore()

    def greet(frame, tile):
        pl.semaphore_signal(
            barrier, inc=1, device_id={"frame": frame, "tile": tile},
            device_id_type=pl.DeviceIdType.MESH,
        )

    for frame in (partner, across, diagonal):
        greet(frame, t)
    for ok, tile in ((has_up, t - 1), (has_down, t + 1)):

        @pl.when(ok)
        def _(tile=tile):
            greet(f, tile)
            greet(partner, tile)

    def remote(name, src, dst, frame, tile):
        return pltpu.make_async_remote_copy(
            src_ref=src, dst_ref=dst, send_sem=send_sem.at[SLOT[name]], recv_sem=recv_sem.at[SLOT[name]],
            device_id={"frame": frame, "tile": tile}, device_id_type=pl.DeviceIdType.MESH,
        )

    def here(name, src, dst):
        return pltpu.make_async_copy(src, dst, local_sem.at[LSLOT[name]])

    @pl.when(jnp.logical_not(has_halo))
    def _():
        for ref in (e, h, f2, h2):
            ref[pl.ds(2 * half * core, half)] = jnp.zeros(
                (half,) + ref.shape[1:], ref.dtype
            )

    pl.semaphore_wait(barrier, 3 + 2 * has_up.astype(jnp.int32) + 2 * has_down.astype(jnp.int32))

    cut = (slice(0, block + LANES), slice(block + LANES, width))
    mine = slice(half, 2 * half)

    def downs(k):
        return remote(f"down{k}", own.at[half:, :, cut[k]], e.at[:half, :, cut[k]], f, t + 1)

    def ups(k):
        return remote(f"up{k}", own.at[:half, :, cut[k]], e.at[2 * half :, :, cut[k]], partner, t - 1)

    def evens(k):
        return remote(f"even{k}", own.at[:, :, cut[k]], e.at[: 2 * half, :, cut[k]], partner, t)

    odd = remote("odd", own.at[:half], b1, partner, t)
    own_copy = here("own", own, e.at[half:])
    base_copy = here("base", own.at[half:], b1)

    @pl.when(is_even)
    def _():
        for k in range(2):
            @pl.when(has_down)
            def _():
                downs(k).start()

            @pl.when(has_up)
            def _():
                ups(k).start()

            evens(k).start()
        own_copy.start()

    @pl.when(is_odd)
    def _():
        odd.start()
        base_copy.start()

    build_weights(pw, 0, wa)
    build_weights(uw, 0, wb)
    build_weights(pw, 1, wc)
    build_weights(uw, 1, wd)

    def network(src, base, dst, cols, keep, w_ref, b_ref, level, sign, await_halo):
        size = cols.stop - cols.start
        column = lax.broadcasted_iota(jnp.int32, (1, size), 1)
        first, final = column == 0, column == size - 1
        hidden = (a_ref, c_ref, d_ref)

        def phase_step(phase, carry):
            @pl.when(phase == 1)
            def _():
                await_halo()

            source = src
            for layer in range(layers):
                count = (src.shape[0] - 2 * (layer + 1)) // 2
                free = max(half - (layer + 1), 0)
                last = layer == layers - 1
                target = dst if last else hidden[layer]

                def pair(i, carry, source=source, target=target, layer=layer, last=last):
                    span = cols if layer == 0 else slice(0, size)
                    x = source[pl.ds(2 * i, 4), :, span].reshape(4 * channels, size)
                    acc = jnp.dot(w_ref[layer], x, preferred_element_type=jnp.float32)
                    group = 2 * channels
                    left = pltpu.roll(acc[:group], 1, 1)
                    right = pltpu.roll(acc[2 * group :], size - 1, 1)
                    y = (
                        acc[group : 2 * group]
                        + jnp.where(first, 0.0, left)
                        + jnp.where(final, 0.0, right)
                        + b_ref[level, layer]
                    )
                    for p in range(2):
                        value = y[p * channels : (p + 1) * channels]
                        if last:
                            value = value[:, keep.start - cols.start : keep.stop - cols.start]
                            old = base[2 * i + p, :, keep].astype(jnp.float32)
                            value = old + value if sign > 0 else old - value
                            target[2 * i + p, :, keep] = value.astype(jnp.bfloat16)
                        else:
                            g = first_row + layer + 1 + 2 * i + p
                            inside = jnp.logical_and(g >= 0, g < tiles * own_rows)
                            value = jnp.where(inside, jnp.maximum(value, 0.0), 0.0)
                            target[2 * i + p, :, 0:size] = value.astype(jnp.bfloat16)
                    return carry

                begin = (1 - phase) * (1 - core) * (count - free) + phase * core * free
                amount = (1 - phase) * free + phase * (count - free)
                lax.fori_loop(begin, begin + amount, pair, 0)
                source = target
            return carry

        lax.fori_loop(0, 2, phase_step, 0)

    def swap(name, field, cols):
        piece = field.at[mine, :, cols]
        return remote(name, piece, field.at[pl.ds(2 * half * core, half), :, cols], partner, t)

    def swap_in(name, field, cols):
        piece = field.at[mine, :, cols]
        return remote(name, piece, field.at[pl.ds(2 * half * (1 - core), half), :, cols], partner, t)

    def halo(name, field, cols):
        piece = field.at[mine, :, cols]
        return remote(name, piece, field.at[pl.ds(2 * half * (1 - core), half), :, cols], partner, halo_tile)

    def halo_in(name, field, cols):
        piece = field.at[mine, :, cols]
        return remote(name, piece, field.at[pl.ds(2 * half * core, half), :, cols], partner, halo_tile)

    def share(kind, k, field, cols):
        @pl.when(has_halo)
        def _():
            halo(kind + "h" + k, field, cols).start()

        swap(kind + "s" + k, field, cols).start()

    def arrive_halo(kind, k, field, cols):
        @pl.when(has_halo)
        def _():
            halo_in(kind + "h" + k, field, cols).wait_recv()

    def sent(kind, k, field, cols):
        swap(kind + "s" + k, field, cols).wait_send()

        @pl.when(has_halo)
        def _():
            halo(kind + "h" + k, field, cols).wait_send()

    hcut = (slice(0, block), slice(block, width))
    for k in range(2):
        @pl.when(is_even)
        def _():
            if k == 0:
                own_copy.wait()
                odd.wait_recv()

        @pl.when(is_odd)
        def _():
            if k == 0:
                base_copy.wait()
            evens(k).wait_recv()

        def frame_halo(k=k):
            @pl.when(jnp.logical_and(is_even, has_up))
            def _():
                downs(k).wait_recv()

            @pl.when(jnp.logical_and(is_odd, has_down))
            def _():
                ups(k).wait_recv()

        reads = slice(0, block + LANES) if k == 0 else slice(part, width)
        network(e, b1, h.at[mine], reads, hcut[k], wa, pb, 0, -1, frame_halo)
        share("h", str(k), h, hcut[k])

    left, right = slice(0, block), slice(width - block, width)
    near, far = slice(0, part), slice(part, width)
    rest = slice(part, block)
    tail = slice(block - part, block)
    give_near = remote("x", low.at[:, :, near], f2.at[mine, :, near], across, t)
    give_rest = remote("x2", low.at[:, :, rest], f2.at[mine, :, rest], across, t)
    give_odd = remote("x3", low.at[:, :, right], o2, across, t)
    keep_even = here("keep", low.at[:, :, right], f2.at[mine])
    keep_odd = here("keep", low.at[:, :, left], o2)
    for k in range(2):
        swap_in("hs" + str(k), h, hcut[k]).wait_recv()
        reads = slice(0, block) if k == 0 else slice(width - block, width)

        def high_halo(k=k):
            arrive_halo("h", str(k), h, hcut[k])

        network(h, e.at[mine], low, reads, (near, far)[k], wb, ub, 0, 1, high_halo)

        @pl.when(is_lower)
        def _():
            (give_near, give_rest)[k].start()

    high_out = here("out", h.at[: 2 * half], out)
    every = slice(0, block)

    @pl.when(is_lower)
    def _():
        keep_even.start()
        keep_even.wait()

    @pl.when(is_upper)
    def _():
        give_odd.start()
        keep_odd.start()
        give_near.wait_recv()
        give_rest.wait_recv()

    share("f", "", f2, every)

    @pl.when(is_odd)
    def _():
        high_out.start()

    @pl.when(is_lower)
    def _():
        give_odd.wait_recv()

    @pl.when(is_upper)
    def _():
        keep_odd.wait()

    swap_in("fs", f2, every).wait_recv()
    network(f2, o2, h2.at[mine], every, every, wc, pb, 1, -1, lambda: arrive_halo("f", "", f2, every))
    share("g", "", h2, every)
    swap_in("gs", h2, every).wait_recv()

    high_send = remote("hl", h2.at[half:, :, tail], out.at[:, :, far], across, t)
    high_keep = here("out", h2.at[half:, :, near], out.at[:, :, near])
    at_low = jnp.logical_and(is_even, is_lower)
    at_high = jnp.logical_and(is_even, is_upper)

    @pl.when(at_low)
    def _():
        high_send.start()

    @pl.when(at_high)
    def _():
        high_keep.start()

    network(h2, f2.at[mine], l2, every, every, wd, ub, 1, 1, lambda: arrive_halo("g", "", h2, every))

    low_keep = here("out2", l2.at[:, :, tail], out.at[:half, :, far])
    first = remote("l1", l2.at[:, :, tail], out.at[half:, :, far], partner, t)
    second = remote("l2", l2.at[:, :, near], out.at[:half, :, near], across, t)
    third = remote("l3", l2.at[:, :, near], out.at[half:, :, near], diagonal, t)

    @pl.when(at_low)
    def _():
        low_keep.start()
        first.wait_recv()
        second.wait_recv()
        third.wait_recv()
        low_keep.wait()
        high_send.wait_send()

    @pl.when(at_high)
    def _():
        second.start()
        high_keep.wait()
        high_send.wait_recv()
        second.wait_send()

    @pl.when(jnp.logical_and(is_odd, is_lower))
    def _():
        first.start()
        first.wait_send()

    @pl.when(jnp.logical_and(is_odd, is_upper))
    def _():
        third.start()
        third.wait_send()

    @pl.when(is_odd)
    def _():
        high_out.wait()
        odd.wait_send()

    @pl.when(is_even)
    def _():
        for k in range(2):
            @pl.when(has_down)
            def _():
                downs(k).wait_send()

            @pl.when(has_up)
            def _():
                ups(k).wait_send()

            evens(k).wait_send()

    @pl.when(is_lower)
    def _():
        give_near.wait_send()
        give_rest.wait_send()

    @pl.when(is_upper)
    def _():
        give_odd.wait_send()

    for k in range(2):
        sent("h", str(k), h, hcut[k])
    sent("f", "", f2, every)
    sent("g", "", h2, every)


def local(frames, predict_w, predict_b, update_w, update_b):
    own = jnp.transpose(frames[0], (1, 0, 2))
    own_rows, channels, width = own.shape
    half = own_rows // 2
    layers = predict_w.shape[1]
    block = width // 2 + LANES
    tiles = lax.axis_size("tile")

    def wide_bias(b):
        return jnp.concatenate([b, b], axis=-1)[..., None]

    vmem = pl.BlockSpec(memory_space=pltpu.VMEM)
    hbm = pl.BlockSpec(memory_space=pl.ANY)

    def buffer(rows, columns):
        return pltpu.VMEM((rows, channels, columns), jnp.bfloat16)

    weight = pltpu.VMEM((layers, 6 * channels, 4 * channels), jnp.bfloat16)
    result = pl.pallas_call(
        functools.partial(kernel, tiles),
        out_shape=jax.ShapeDtypeStruct(own.shape, jnp.bfloat16),
        in_specs=[hbm, vmem, vmem, vmem, vmem],
        out_specs=hbm,
        scratch_shapes=[
            buffer(3 * half, width), buffer(3 * half, width), buffer(half, width), buffer(half, width),
            buffer(3 * half, block), buffer(3 * half, block), buffer(half, block), buffer(half, block),
            weight, weight, weight, weight,
            buffer(3 * half - 2, block + LANES), buffer(3 * half - 4, block + LANES),
            buffer(3 * half - 6, block + LANES),
            pltpu.SemaphoreType.DMA((len(MESSAGES),)),
            pltpu.SemaphoreType.DMA((len(MESSAGES),)),
            pltpu.SemaphoreType.DMA((len(LOCAL),)),
        ],
        compiler_params=pltpu.CompilerParams(
            collective_id=0, has_side_effects=True, vmem_limit_bytes=60 * 1024 * 1024
        ),
    )(own, predict_w, update_w, wide_bias(predict_b), wide_bias(update_b))
    return jnp.transpose(result, (1, 0, 2))[None]


def solution(mesh):
    in_specs = (P("frame", None, "tile", None), P(), P(), P(), P())
    out_specs = P("frame", None, "tile", None)
    return jax.shard_map(local, mesh=mesh, in_specs=in_specs, out_specs=out_specs, check_vma=False)
```

profile of v0, /device:TPU:0, one launch (start us, length us, event | category | flops | bytes accessed | tf_op | source)
XLA Modules:
  0.0 122.4 jit_solution(12970255008505068588)
XLA Ops:
  0.0 0.8 maximum_bitcast_fusion
  0.8 0.8 maximum_bitcast_fusion.1
  1.7 1.0 copy.10.ub
  2.7 1.0 copy.9.pb
  3.8 4.1 %copy.13 = bf16[1,64,8,2048]{3,1,2,0:T(8,128)(2,1)} copy(bf16[1,64,8,2048]{3,2,1,0:T(8,128)(2,1)} %param.5) | data formatting | bytes 4194304 | tf_op args[0]
  7.8 110.5 %shard_map.55 = bf16[8,64,2048]{2,1,0:T(8,128)(2,1)} custom-call(bf16[8,64,2048]{2,1,0:T(8,128)(2,1)} %bitcast.13, bf16[2,4,3,3,64,64]{5,4,3,2,1,0:T(8,128)(2,1)} %pw.1, bf16[2,4,3,3,64,64]{5,4,3,2,1,0:T(8,128)(2,1)} %uw.1, f32[2,4,128,1]{3,2,1,0:T(8,128)} %copy.9.pb, f32[2,4,128,1]{3,2,1,0:T(8,128)} %copy.10.ub), custom_call_target="tpu_custom_call" | custom-call | tf_op jit(solution)/shard_map/pallas_call | solution.py:397
  118.3 4.1 %copy.11 = bf16[1,64,8,2048]{3,2,1,0:T(8,128)(2,1)} copy(bf16[1,64,8,2048]{3,1,2,0:T(8,128)(2,1)} %bitcast.12) | data formatting | bytes 4194304 | tf_op jit(solution)/shard_map/broadcast_in_dim | solution.py:416
where the time goes:
time: 123 us; the launch traced here: 122 us
  Pallas kernels  110 us (89%)
  local copies, waits for them, and re-layouts  10.2 us (8%)
  other arithmetic  1.67 us (1%)
    pallas_call x1, Pallas kernels, local(): pl.pallas_call(functools.partial(kernel, tiles), out_shape=jax.ShapeDtype...  110 us
    broadcast_in_dim x1, local copies, waits for them, and re-layouts, local(): return jnp.transpose(result, (1, 0, 2))[None]  4.06 us
    unnamed x1, local copies, waits for them, and re-layouts  4.06 us

commit v1 on v0

v1 whole, which is shorter than its diff:
```python
import functools

import jax
import jax.numpy as jnp
from jax import lax
from jax.experimental import pallas as pl
from jax.experimental.pallas import tpu as pltpu
from jax.sharding import PartitionSpec as P

LANES = 128
HALF_LANES = LANES // 2
PEERS = ((0, 1), (1, 0), (1, 1), (0, 0))
EDGES = ("e0", "e1", "h0", "h1", "f", "g")
RECV, SEND = {}, {}
for _kind in ("main", "pad"):
    for _c in range(2):
        for _dx in range(2):
            RECV[_kind, _c, _dx] = len(RECV)
for _k in range(8):
    RECV["out", _k] = len(RECV)
for _e in EDGES:
    for _side in ("inner", "outer"):
        RECV[_e, _side] = len(RECV)
for _kind in ("main", "pad"):
    for _p in PEERS:
        SEND[_kind, _p] = len(SEND)
for _name in ("high0", "high1", "high2", "low2"):
    for _k in range(2):
        SEND[_name, _k] = len(SEND)
for _e in EDGES:
    for _side in ("inner", "outer"):
        SEND[_e, _side] = len(SEND)


def flip(v, d):
    return v + d - 2 * v * d


def kernel(tiles, own, pw, uw, pb, ub, out, e, o, h, fb, g2, l2, a_ref, c_ref, d_ref, acc0, acc1, wa, wb, wc, wd,
           bias, cuts, pads, send_sem, recv_sem, local_sem):
    rows, channels, width = own.shape
    layers = pw.shape[1]
    block = width // 4
    span = block + LANES
    edge = rows // 2
    f = lax.axis_index("frame")
    t = lax.axis_index("tile")
    core, x = lax.rem(f, 2), lax.div(f, 2)
    y, slab = lax.rem(t, 2), lax.div(t, 2)
    slabs = tiles // 2
    first_tile = t - y
    partner = f + 1 - 2 * core
    q = 2 * x + y
    is_even, is_odd = core == 0, core == 1
    outer_slab = slab + 2 * core - 1
    has_outer = jnp.logical_and(outer_slab >= 0, outer_slab < slabs)
    outer_tile = t + 4 * core - 2
    me_local = y == core

    def cols(k, size=block):
        return pl.ds(pl.multiple_of(k * block, LANES), size)

    barrier = pltpu.get_barrier_semaphore()

    def greet(frame, tile):
        pl.semaphore_signal(
            barrier, inc=1, device_id={"frame": frame, "tile": tile}, device_id_type=pl.DeviceIdType.MESH,
        )

    for dx in range(2):
        for dc in range(2):
            for dy in range(2):
                if dx or dc or dy:
                    greet(2 * flip(x, dx) + flip(core, dc), first_tile + flip(y, dy))

    @pl.when(has_outer)
    def _():
        greet(partner, outer_tile)

    def remote(src, dst, send, recv, frame, tile):
        return pltpu.make_async_remote_copy(
            src_ref=src, dst_ref=dst, send_sem=send_sem.at[send], recv_sem=recv_sem.at[recv],
            device_id={"frame": frame, "tile": tile}, device_id_type=pl.DeviceIdType.MESH,
        )

    cut_copies = [
        pltpu.make_async_copy(
            own.at[:, :, k * block + block - LANES : k * block + block + LANES], cuts.at[k], local_sem.at[k]
        )
        for k in range(3)
    ]
    for copy in cut_copies:
        copy.start()

    @pl.when(jnp.logical_not(has_outer))
    def _():
        zero = jnp.zeros((edge, channels, span), jnp.bfloat16)
        at = pl.ds(3 * edge * core, edge)
        for v in range(3):
            for d in range(2):
                e[v, d, at] = zero
                h[v, d, at] = zero
            fb[0, v, at] = zero
            g2[v, at] = zero

    pl.semaphore_wait(barrier, 7 + has_outer.astype(jnp.int32))

    mine = slice(edge, edge + rows)

    def landing(c, dx, part):
        at = slice(0, block) if part == "main" else slice(block, span)
        return e.at[1, dx, mine, :, at] if c == 0 else o.at[dx, :, :, at]

    def parcel(c, peer, part):
        dx, dy = peer
        px, py = flip(x, dx), flip(y, dy)
        pq = 2 * px + py
        src = own.at[:, :, cols(pq)] if part == "main" else pads.at[pq]
        return src, landing(c, dx, part), 2 * px + y, first_tile + py

    def ship(c, peer, part, action):
        src, dst, frame, tile = parcel(c, peer, part)
        copy = remote(src, dst, SEND[part, peer], RECV[part, c, peer[0]], frame, tile)
        if peer != (0, 0):
            action(copy)
        else:
            same = y == c

            @pl.when(jnp.logical_not(same))
            def _():
                action(copy)

            @pl.when(same)
            def _():
                action(pltpu.make_async_copy(src, dst, local_sem.at[3 if part == "main" else 4]))

    def start(copy):
        copy.start()

    def settle(copy):
        if copy.is_remote:
            copy.wait_send()

    def arrive(c, dx):
        for part in ("main", "pad"):
            src, dst, frame, tile = parcel(c, (dx, 0), part)
            copy = remote(src, dst, SEND[part, (dx, 0)], RECV[part, c, dx], frame, tile)
            if dx:
                copy.wait_recv()
            else:
                local = jnp.logical_and(me_local, core == c)

                @pl.when(jnp.logical_not(local))
                def _(copy=copy):
                    copy.wait_recv()

                @pl.when(local)
                def _(src=src, dst=dst, part=part):
                    pltpu.make_async_copy(src, dst, local_sem.at[3 if part == "main" else 4]).wait()

    @pl.when(is_even)
    def _():
        for peer in ((0, 1), (1, 0), (0, 0)):
            ship(0, peer, "main", start)

    @pl.when(is_odd)
    def _():
        ship(1, (0, 0), "main", start)

    lane = lax.broadcasted_iota(jnp.int32, (1, 1, LANES), 2)
    for copy in cut_copies:
        copy.wait()
    nothing = jnp.zeros((rows, channels, LANES), jnp.float32)
    for k in range(4):
        right = cuts[k, :, :, LANES:].astype(jnp.float32) if k < 3 else nothing
        left = cuts[k - 1, :, :, :LANES].astype(jnp.float32) if k > 0 else nothing
        pads[k] = jnp.where(lane < HALF_LANES, right, left).astype(jnp.bfloat16)

    @pl.when(is_even)
    def _():
        for peer in ((0, 1), (1, 0), (0, 0)):
            ship(0, peer, "pad", start)
        for part in ("main", "pad"):
            ship(0, (1, 1), part, start)

    @pl.when(is_odd)
    def _():
        ship(1, (0, 0), "pad", start)

    def build(k_ref, level, w_ref):
        for layer in range(layers):
            w_ref[layer] = jnp.zeros(w_ref.shape[1:], w_ref.dtype)
            for p in range(2):
                for s in range(3):
                    for r in range(3):
                        at = 4 * channels * s + channels * (r + p)
                        w_ref[layer, p * channels : (p + 1) * channels, at : at + channels] = k_ref[level, layer, r, s]

    def spread_bias(b_ref, level, base):
        row = lax.broadcasted_iota(jnp.int32, (channels, channels), 0)
        col = lax.broadcasted_iota(jnp.int32, (channels, channels), 1)
        for layer in range(layers):
            values = jnp.where(row == col, b_ref[level, layer : layer + 1, :], 0.0)
            column = jnp.sum(values, axis=1, keepdims=True)
            full = jnp.broadcast_to(column, (channels, LANES))
            bias[base + layer, :channels] = full
            bias[base + layer, channels:] = full

    for k, (k_ref, b_ref, level, w_ref) in enumerate(
        ((pw, pb, 0, wa), (uw, ub, 0, wb), (pw, pb, 1, wc), (uw, ub, 1, wd))
    ):
        build(k_ref, level, w_ref)
        spread_bias(b_ref, level, k * layers)
    arrive(0, 0)

    @pl.when(is_odd)
    def _():
        for peer in ((0, 1), (1, 0), (1, 1)):
            for part in ("main", "pad"):
                ship(1, peer, part, start)

    lane2 = lax.broadcasted_iota(jnp.int32, (1, LANES), 1)
    in_frame = jnp.logical_or(
        jnp.logical_and(lane2 < HALF_LANES, q < 3), jnp.logical_and(lane2 >= HALF_LANES, q > 0)
    )

    def clip(value):
        return jnp.concatenate([value[:, :block], jnp.where(in_frame, value[:, block:], 0.0)], axis=1)

    def step(index):
        return 0 if index is None else 2 * index

    def edge_copy(name, side, field, index):
        if side == "inner":
            src, dst, tile = edge * (2 - core), 3 * edge * core, t
        else:
            src, dst, tile = edge * (1 + core), 3 * edge * (1 - core), outer_tile
        lead = (1,) if index is None else (1, index)
        return remote(
            field.at[lead + (pl.ds(src, edge),)], field.at[lead + (pl.ds(dst, edge),)],
            SEND[name, side] + step(index), RECV[name, side] + step(index), partner, tile,
        )

    def edge_in(name, side, field, index):
        if side == "inner":
            at, tile = 3 * edge * (1 - core), t
        else:
            at, tile = 3 * edge * core, outer_tile
        lead = (1,) if index is None else (1, index)
        piece = field.at[lead + (pl.ds(at, edge),)]
        return remote(piece, piece, SEND[name, side] + step(index), RECV[name, side] + step(index), partner, tile), at

    def send_edge(name, side, field, index=None):
        if side == "inner":
            edge_copy(name, side, field, index).start()
        else:
            @pl.when(has_outer)
            def _():
                edge_copy(name, side, field, index).start()

    def edge_sent(name, field, index=None):
        edge_copy(name, "inner", field, index).wait_send()

        @pl.when(has_outer)
        def _():
            edge_copy(name, "outer", field, index).wait_send()

    def turn(field, lead, at, count):
        for k in range(count):
            value = field[(1,) + lead + (at + k,)]
            field[(0,) + lead + (at + k,)] = pltpu.roll(value, 1, 1)
            field[(2,) + lead + (at + k,)] = pltpu.roll(value, span - 1, 1)

    hidden = (a_ref, c_ref, d_ref)

    def run_steps(steps):
        accs = (acc0, acc1)
        waiting = None
        for k, (mm, post, layer, offset) in enumerate(steps):
            if waiting is not None and waiting[1] < layer and waiting[2] < offset + 6 and offset < waiting[2] + 4:
                waiting[0](accs[(k - 1) % 2])
                waiting = None
            mm(accs[k % 2])
            if waiting is not None:
                waiting[0](accs[(k - 1) % 2])
            waiting = post, layer, offset
        waiting[0](accs[(len(steps) - 1) % 2])

    def network(read, w_ref, base, finish, outer_phase):
        steps = []
        for layer in range(layers):
            total = 2 * rows - 2 * (layer + 1)
            last = layer == layers - 1
            if outer_phase:
                count, begin = edge, core * (total - edge)
            else:
                count, begin = total - edge, edge * (1 - core)
            offsets = sorted({min(k, count - 4) for k in range(0, count, 4)})
            source = read if layer == 0 else (lambda s, at, ref=hidden[layer - 1]: ref[s, at])
            for offset in offsets:
                j = begin + offset

                def mm(acc, j=j, source=source, layer=layer):
                    parts = []
                    for s in range(3):
                        parts.append(jnp.concatenate(
                            [source(s, pl.ds(j + 2 * k, 4)).reshape(4 * channels, span) for k in range(2)], axis=1
                        ))
                    stack = jnp.concatenate(parts, axis=0)
                    acc[...] = jnp.dot(w_ref[layer], stack, preferred_element_type=jnp.float32)

                def post(acc, j=j, layer=layer, last=last):
                    shift = jnp.concatenate([bias[base + layer]] * (span // LANES), axis=1)
                    for k in range(2):
                        value = acc[:, k * span : (k + 1) * span] + shift
                        if last:
                            finish(j + 2 * k, value)
                            continue
                        value = jnp.maximum(value, 0.0)
                        if outer_phase:
                            halves = []
                            for p in range(2):
                                i = 2 * k + p
                                outside = jnp.logical_and(
                                    jnp.logical_not(has_outer),
                                    jnp.logical_or(
                                        jnp.logical_and(is_even, i < layers - 1 - layer),
                                        jnp.logical_and(is_odd, i > layer),
                                    ),
                                )
                                halves.append(jnp.where(outside, 0.0, value[p * channels : (p + 1) * channels]))
                            value = jnp.concatenate(halves, axis=0)
                        emit(hidden[layer], (), j + 2 * k, value)

                steps.append((mm, post, layer, offset))
        run_steps(steps)

    def emit(ref, lead, j, value, versions=(0, 1, 2)):
        packed = clip(value).astype(jnp.bfloat16)
        for v in versions:
            turned = packed if v == 1 else pltpu.roll(packed, 1 if v == 0 else span - 1, 1)
            for p in range(2):
                ref[(v,) + lead + (j + p,)] = turned[p * channels : (p + 1) * channels]

    def pair_of(values):
        return jnp.concatenate([values[0], values[1]], axis=0).astype(jnp.float32)

    def field_network(name, field, index, w_ref, base, finish, after_inner):
        lead = () if index is None else (index,)
        read = lambda s, at: field[(s,) + lead + (at,)]
        copy, at = edge_in(name, "inner", field, index)
        copy.wait_recv()
        turn(field, lead, at, edge)
        network(read, w_ref, base, finish, False)
        after_inner()
        copy, at = edge_in(name, "outer", field, index)

        @pl.when(has_outer)
        def _():
            copy.wait_recv()
            turn(field, lead, at, edge)

        network(read, w_ref, base, finish, True)

    def out_copy(name, half, source, frame, dx, d):
        at = edge * (1 - core) if half == 0 else edge * core
        dy = flip(y, core)
        src = source(at)
        dst = out.at[pl.ds(at, edge), :, cols(q)]
        return remote(src, dst, SEND[name, half] + 2 * d, RECV["out", 0] + 4 * dx + 2 * dy + half, frame, first_tile + core), (
            lambda: pltpu.make_async_copy(src, dst, local_sem.at[5 + half])
        )

    def deliver(name, half, source, frame, dx, action, d=0):
        copy, local = out_copy(name, half, source, frame, dx, d)
        mine_only = jnp.logical_and(f == frame, me_local)

        @pl.when(jnp.logical_not(mine_only))
        def _():
            action(copy)

        @pl.when(mine_only)
        def _():
            action(local())

    def high_piece(d):
        return lambda at: h.at[1, d, pl.ds(edge + at, edge), :, 0:block]

    turn(e, (0,), edge, rows)
    send_edge("e0", "inner", e, 0)
    send_edge("e0", "outer", e, 0)
    def pair_network(d, carry):
        p_index = flip(x, d)

        @pl.when(d == 1)
        def _():
            arrive(0, 1)
            send_edge("e0", "inner", e, d)
            send_edge("e0", "outer", e, d)
            turn(e, (d,), edge, rows)

        def high(j, value):
            old = pair_of([o[d, j], o[d, j + 1]])
            emit(h, (d,), edge + j, old - value)

        def high_inner():
            send_edge("h0", "inner", h, d)
            deliver("high0", 0, high_piece(d), 2 * p_index + 1, d, start, d)

        for dx in range(2):
            @pl.when(d == dx)
            def _(dx=dx):
                arrive(1, dx)

        field_network("e0", e, d, wa, 0, high, high_inner)
        send_edge("h0", "outer", h, d)
        deliver("high0", 1, high_piece(d), 2 * p_index + 1, d, start, d)

        def low(j, value):
            old = pair_of([e[1, d, edge + j], e[1, d, edge + j + 1]])
            packed = clip(old + value).astype(jnp.bfloat16)
            for v in range(3):
                turned = packed if v == 1 else pltpu.roll(packed, 1 if v == 0 else span - 1, 1)
                for p in range(2):
                    fb[p_index, v, edge + j + p] = turned[p * channels : (p + 1) * channels]

        def low_inner():
            @pl.when(x == d)
            def _():
                send_edge("f", "inner", fb.at[0])

        field_network("h0", h, d, wb, layers, low, low_inner)

        @pl.when(x == d)
        def _():
            send_edge("f", "outer", fb.at[0])

        return carry

    lax.fori_loop(0, 2, pair_network, 0)

    def high_two(j, value):
        old = pair_of([fb[1, 1, edge + j], fb[1, 1, edge + j + 1]])
        emit(g2, (), edge + j, old - value)

    def g_piece(at):
        return g2.at[1, pl.ds(edge + at, edge), :, 0:block]

    def g_inner():
        send_edge("g", "inner", g2)
        deliver("high2", 0, g_piece, 2, 1 - x, start)

    field_network("f", fb.at[0], None, wc, 2 * layers, high_two, g_inner)
    send_edge("g", "outer", g2)
    deliver("high2", 1, g_piece, 2, 1 - x, start)

    def low_two(j, value):
        old = pair_of([fb[0, 1, edge + j], fb[0, 1, edge + j + 1]])
        packed = (old + value)[:, :block].astype(jnp.bfloat16)
        for p in range(2):
            l2[j + p] = packed[p * channels : (p + 1) * channels]

    def l_piece(at):
        return l2.at[pl.ds(at, edge)]

    def l_inner():
        deliver("low2", 0, l_piece, 0, x, start)

    field_network("g", g2, None, wd, 3 * layers, low_two, l_inner)
    deliver("low2", 1, l_piece, 0, x, start)

    for dx in range(2):
        for dy in range(2):
            for half in range(2):
                rows_at = edge * (1 - y) if half == 0 else edge * y
                dst = out.at[pl.ds(rows_at, edge), :, cols(2 * flip(x, dx) + flip(y, dy))]
                copy = remote(dst, dst, 0, RECV["out", 0] + 4 * dx + 2 * dy + half, partner, t)
                if dx or dy:
                    copy.wait_recv()
                else:
                    @pl.when(jnp.logical_not(me_local))
                    def _(copy=copy):
                        copy.wait_recv()

                    @pl.when(me_local)
                    def _(dst=dst, half=half):
                        pltpu.make_async_copy(dst, dst, local_sem.at[5 + half]).wait()

    for c, flag in ((0, is_even), (1, is_odd)):
        @pl.when(flag)
        def _(c=c):
            for peer in PEERS:
                for part in ("main", "pad"):
                    ship(c, peer, part, settle)
    for d in range(2):
        edge_sent("e0", e, d)
        edge_sent("h0", h, d)
        for half in range(2):
            deliver("high0", half, high_piece(d), 2 * flip(x, d) + 1, d, settle, d)
    edge_sent("f", fb.at[0])
    edge_sent("g", g2)
    for half in range(2):
        deliver("high2", half, g_piece, 2, 1 - x, settle)
        deliver("low2", half, l_piece, 0, x, settle)


def local(frames, predict_w, predict_b, update_w, update_b):
    own = jnp.transpose(frames[0], (1, 0, 2))
    rows, channels, width = own.shape
    layers = predict_w.shape[1]
    block = width // 4
    span = block + LANES
    tiles = lax.axis_size("tile")
    vmem = pl.BlockSpec(memory_space=pltpu.VMEM)
    hbm = pl.BlockSpec(memory_space=pl.ANY)

    def buffer(*lead, columns=span):
        return pltpu.VMEM(lead + (channels, columns), jnp.bfloat16)

    weight = pltpu.VMEM((layers, 2 * channels, 12 * channels), jnp.bfloat16)
    acc = pltpu.VMEM((2 * channels, 2 * span), jnp.float32)
    result = pl.pallas_call(
        functools.partial(kernel, tiles),
        out_shape=jax.ShapeDtypeStruct(own.shape, jnp.bfloat16),
        in_specs=[hbm, vmem, vmem, vmem, vmem],
        out_specs=hbm,
        scratch_shapes=[
            buffer(3, 2, 2 * rows), buffer(2, rows), buffer(3, 2, 2 * rows), buffer(2, 3, 2 * rows),
            buffer(3, 2 * rows), buffer(rows, columns=block),
            buffer(3, 2 * rows - 2), buffer(3, 2 * rows - 4), buffer(3, 2 * rows - 6),
            acc, acc, weight, weight, weight, weight,
            pltpu.VMEM((4 * layers, 2 * channels, LANES), jnp.float32),
            buffer(3, rows, columns=2 * LANES), buffer(4, rows, columns=LANES),
            pltpu.SemaphoreType.DMA((len(SEND),)),
            pltpu.SemaphoreType.DMA((len(RECV),)),
            pltpu.SemaphoreType.DMA((7,)),
        ],
        compiler_params=pltpu.CompilerParams(
            collective_id=0, has_side_effects=True, vmem_limit_bytes=60 * 1024 * 1024
        ),
    )(own, predict_w, update_w, predict_b, update_b)
    return jnp.transpose(result, (1, 0, 2))[None]


def solution(mesh):
    in_specs = (P("frame", None, "tile", None), P(), P(), P(), P())
    out_specs = P("frame", None, "tile", None)
    return jax.shard_map(local, mesh=mesh, in_specs=in_specs, out_specs=out_specs, check_vma=False)
```

time: 123 us -> 101 us (0.82)
  the two profiles are of different devices: /device:TPU:0 before, /device:TPU:16 now
where the time goes in v1:
time: 101 us; the launch traced here: 100 us
  Pallas kernels  92.4 us (91%)
  local copies, waits for them, and re-layouts  8.12 us (8%)
    pallas_call x1, Pallas kernels, local(): pl.pallas_call(functools.partial(kernel, tiles), out_shape=jax.ShapeDtype...  92.4 us
    broadcast_in_dim x1, local copies, waits for them, and re-layouts, local(): return jnp.transpose(result, (1, 0, 2))[None]  4.06 us
    unnamed x1, local copies, waits for them, and re-layouts  4.06 us

profile of v1, /device:TPU:16, one launch (start us, length us, event | category | flops | bytes accessed | tf_op | source)
XLA Modules:
  0.0 100.5 jit_solution(14654160180910098874)
XLA Ops:
  0.0 4.1 %copy.9 = bf16[1,64,8,2048]{3,1,2,0:T(8,128)(2,1)} copy(bf16[1,64,8,2048]{3,2,1,0:T(8,128)(2,1)} %param.5) | data formatting | bytes 4194304 | tf_op args[0]
  4.1 92.4 %shard_map.55 = bf16[8,64,2048]{2,1,0:T(8,128)(2,1)} custom-call(bf16[8,64,2048]{2,1,0:T(8,128)(2,1)} %bitcast.9, bf16[2,4,3,3,64,64]{5,4,3,2,1,0:T(8,128)(2,1)} %pw.1, bf16[2,4,3,3,64,64]{5,4,3,2,1,0:T(8,128)(2,1)} %uw.1, f32[2,4,64]{2,1,0:T(4,128)} %pb.1, f32[2,4,64]{2,1,0:T(4,128)} %ub.1), custom_call_target="tpu_custom_call" | custom-call | tf_op jit(solution)/shard_map/pallas_call | solution.py:522
  96.4 4.1 %copy.7 = bf16[1,64,8,2048]{3,2,1,0:T(8,128)(2,1)} copy(bf16[1,64,8,2048]{3,1,2,0:T(8,128)(2,1)} %bitcast.8) | data formatting | bytes 4194304 | tf_op jit(solution)/shard_map/broadcast_in_dim | solution.py:542

commit v2 on v1

--- a/solution.py
+++ b/solution.py
@@ -37,7 +37,7 @@
 
 
 def kernel(tiles, own, pw, uw, pb, ub, out, e, o, h, fb, g2, l2, a_ref, c_ref, d_ref, acc0, acc1, wa, wb, wc, wd,
-           bias, cuts, pads, send_sem, recv_sem, local_sem):
+           bias, cuts, pads, packs, send_sem, recv_sem, local_sem):
     rows, channels, width = own.shape
     layers = pw.shape[1]
     block = width // 4
@@ -106,10 +106,13 @@
     pl.semaphore_wait(barrier, 7 + has_outer.astype(jnp.int32))
 
     mine = slice(edge, edge + rows)
+    reach = 4 * layers
+    group = LANES // (2 * reach)
 
     def landing(c, dx, part):
-        at = slice(0, block) if part == "main" else slice(block, span)
-        return e.at[1, dx, mine, :, at] if c == 0 else o.at[dx, :, :, at]
+        if part == "pad":
+            return packs.at[c, dx]
+        return e.at[1, dx, mine, :, 0:block] if c == 0 else o.at[dx, :, :, 0:block]
 
     def parcel(c, peer, part):
         dx, dy = peer
@@ -157,6 +160,16 @@
                 @pl.when(local)
                 def _(src=src, dst=dst, part=part):
                     pltpu.make_async_copy(src, dst, local_sem.at[3 if part == "main" else 4]).wait()
+        for unit in range(rows // group):
+            value = packs[c, dx, unit].astype(jnp.float32)
+            for i in range(group):
+                strip = pltpu.roll(value, (-reach - 2 * reach * i) % LANES, 1)
+                strip = jnp.where(jnp.logical_or(lane < reach, lane >= LANES - reach), strip, 0.0).astype(jnp.bfloat16)
+                row = unit * group + i
+                if c == 0:
+                    e[1, dx, edge + row, :, block:span] = strip
+                else:
+                    o[dx, row, :, block:span] = strip
 
     @pl.when(is_even)
     def _():
@@ -165,16 +178,24 @@
 
     @pl.when(is_odd)
     def _():
-        ship(1, (0, 0), "main", start)
-
-    lane = lax.broadcasted_iota(jnp.int32, (1, 1, LANES), 2)
+        for peer in ((0, 1), (1, 0), (0, 0)):
+            ship(1, peer, "main", start)
+
+    lane = lax.broadcasted_iota(jnp.int32, (1, LANES), 1)
     for copy in cut_copies:
         copy.wait()
-    nothing = jnp.zeros((rows, channels, LANES), jnp.float32)
     for k in range(4):
-        right = cuts[k, :, :, LANES:].astype(jnp.float32) if k < 3 else nothing
-        left = cuts[k - 1, :, :, :LANES].astype(jnp.float32) if k > 0 else nothing
-        pads[k] = jnp.where(lane < HALF_LANES, right, left).astype(jnp.bfloat16)
+        for unit in range(rows // group):
+            total = jnp.zeros((channels, LANES), jnp.float32)
+            for i in range(group):
+                row = unit * group + i
+                strip = jnp.zeros((channels, LANES), jnp.float32)
+                if k < 3:
+                    strip = jnp.where(lane < reach, cuts[k, row, :, LANES:].astype(jnp.float32), strip)
+                if k > 0:
+                    strip = jnp.where(lane >= LANES - reach, cuts[k - 1, row, :, :LANES].astype(jnp.float32), strip)
+                total = total + pltpu.roll(strip, (reach + 2 * reach * i) % LANES, 1)
+            pads[k, unit] = total.astype(jnp.bfloat16)
 
     @pl.when(is_even)
     def _():
@@ -185,7 +206,10 @@
 
     @pl.when(is_odd)
     def _():
-        ship(1, (0, 0), "pad", start)
+        for peer in ((0, 1), (1, 0), (0, 0)):
+            ship(1, peer, "pad", start)
+        for part in ("main", "pad"):
+            ship(1, (1, 1), part, start)
 
     def build(k_ref, level, w_ref):
         for layer in range(layers):
@@ -213,15 +237,8 @@
         spread_bias(b_ref, level, k * layers)
     arrive(0, 0)
 
-    @pl.when(is_odd)
-    def _():
-        for peer in ((0, 1), (1, 0), (1, 1)):
-            for part in ("main", "pad"):
-                ship(1, peer, part, start)
-
-    lane2 = lax.broadcasted_iota(jnp.int32, (1, LANES), 1)
     in_frame = jnp.logical_or(
-        jnp.logical_and(lane2 < HALF_LANES, q < 3), jnp.logical_and(lane2 >= HALF_LANES, q > 0)
+        jnp.logical_and(lane < HALF_LANES, q < 3), jnp.logical_and(lane >= HALF_LANES, q > 0)
     )
 
     def clip(value):
@@ -273,67 +290,75 @@
 
     hidden = (a_ref, c_ref, d_ref)
 
-    def run_steps(steps):
+    def plan(counts, outer_phase):
+        if outer_phase:
+            return [(layer, i, 1) for layer in range(layers) for i in range(2)]
+        steps = []
+        for layer, count in enumerate(counts):
+            offset = 0
+            while offset < count:
+                size = 2 if 2 * layer < layers and offset + 4 <= count else 1
+                steps.append((layer, offset, size))
+                offset += 2 * size
+        return steps
+
+    def network(read, w_ref, base, finish, outer_phase, before_last=None):
         accs = (acc0, acc1)
+        totals = [2 * rows - 2 * (layer + 1) for layer in range(layers)]
         waiting = None
-        for k, (mm, post, layer, offset) in enumerate(steps):
-            if waiting is not None and waiting[1] < layer and waiting[2] < offset + 6 and offset < waiting[2] + 4:
-                waiting[0](accs[(k - 1) % 2])
-                waiting = None
-            mm(accs[k % 2])
-            if waiting is not None:
-                waiting[0](accs[(k - 1) % 2])
-            waiting = post, layer, offset
-        waiting[0](accs[(len(steps) - 1) % 2])
-
-    def network(read, w_ref, base, finish, outer_phase):
-        steps = []
-        for layer in range(layers):
-            total = 2 * rows - 2 * (layer + 1)
+        for index, (layer, offset, size) in enumerate(plan([total - edge for total in totals], outer_phase)):
             last = layer == layers - 1
             if outer_phase:
-                count, begin = edge, core * (total - edge)
+                j = core * (totals[layer] - edge) + (2 * core if offset else 2 - 2 * core)
+                clash = False
             else:
-                count, begin = total - edge, edge * (1 - core)
-            offsets = sorted({min(k, count - 4) for k in range(0, count, 4)})
+                j = edge * (1 - core) + offset
+                clash = (
+                    waiting is not None and waiting[1] < layer
+                    and waiting[2] < offset + 2 * size + 2 and offset < waiting[2] + 2 * waiting[3]
+                )
+            if last and before_last is not None:
+                before_last()
+                before_last = None
+            if clash:
+                waiting[0]()
+                waiting = None
+            acc = accs[index % 2]
             source = read if layer == 0 else (lambda s, at, ref=hidden[layer - 1]: ref[s, at])
-            for offset in offsets:
-                j = begin + offset
-
-                def mm(acc, j=j, source=source, layer=layer):
-                    parts = []
-                    for s in range(3):
-                        parts.append(jnp.concatenate(
-                            [source(s, pl.ds(j + 2 * k, 4)).reshape(4 * channels, span) for k in range(2)], axis=1
-                        ))
-                    stack = jnp.concatenate(parts, axis=0)
-                    acc[...] = jnp.dot(w_ref[layer], stack, preferred_element_type=jnp.float32)
-
-                def post(acc, j=j, layer=layer, last=last):
-                    shift = jnp.concatenate([bias[base + layer]] * (span // LANES), axis=1)
-                    for k in range(2):
-                        value = acc[:, k * span : (k + 1) * span] + shift
-                        if last:
-                            finish(j + 2 * k, value)
-                            continue
-                        value = jnp.maximum(value, 0.0)
-                        if outer_phase:
-                            halves = []
-                            for p in range(2):
-                                i = 2 * k + p
-                                outside = jnp.logical_and(
-                                    jnp.logical_not(has_outer),
-                                    jnp.logical_or(
-                                        jnp.logical_and(is_even, i < layers - 1 - layer),
-                                        jnp.logical_and(is_odd, i > layer),
-                                    ),
-                                )
-                                halves.append(jnp.where(outside, 0.0, value[p * channels : (p + 1) * channels]))
-                            value = jnp.concatenate(halves, axis=0)
-                        emit(hidden[layer], (), j + 2 * k, value)
-
-                steps.append((mm, post, layer, offset))
-        run_steps(steps)
+            stack = jnp.concatenate([
+                jnp.concatenate(
+                    [source(s, pl.ds(j + 2 * k, 4)).reshape(4 * channels, span) for k in range(size)], axis=1
+                )
+                for s in range(3)
+            ], axis=0)
+            acc[:, : size * span] = jnp.dot(w_ref[layer], stack, preferred_element_type=jnp.float32)
+            if waiting is not None:
+                waiting[0]()
+
+            def post(acc=acc, j=j, layer=layer, last=last, size=size, offset=offset):
+                shift = jnp.concatenate([bias[base + layer]] * (span // LANES), axis=1)
+                for k in range(size):
+                    value = acc[:, k * span : (k + 1) * span] + shift
+                    if last:
+                        finish(j + 2 * k, value)
+                        continue
+                    value = jnp.maximum(value, 0.0)
+                    if outer_phase:
+                        halves = []
+                        for p in range(2):
+                            outside = jnp.logical_and(
+                                jnp.logical_not(has_outer),
+                                jnp.logical_or(
+                                    jnp.logical_and(is_even, 2 * (1 - offset) + p < layers - 1 - layer),
+                                    jnp.logical_and(is_odd, 2 * offset + p > layer),
+                                ),
+                            )
+                            halves.append(jnp.where(outside, 0.0, value[p * channels : (p + 1) * channels]))
+                        value = jnp.concatenate(halves, axis=0)
+                    emit(hidden[layer], (), j + 2 * k, value)
+
+            waiting = post, layer, offset, size
+        waiting[0]()
 
     def emit(ref, lead, j, value, versions=(0, 1, 2)):
         packed = clip(value).astype(jnp.bfloat16)
@@ -345,13 +370,13 @@
     def pair_of(values):
         return jnp.concatenate([values[0], values[1]], axis=0).astype(jnp.float32)
 
-    def field_network(name, field, index, w_ref, base, finish, after_inner):
+    def field_network(name, field, index, w_ref, base, finish, after_inner, before_last=None):
         lead = () if index is None else (index,)
         read = lambda s, at: field[(s,) + lead + (at,)]
         copy, at = edge_in(name, "inner", field, index)
         copy.wait_recv()
         turn(field, lead, at, edge)
-        network(read, w_ref, base, finish, False)
+        network(read, w_ref, base, finish, False, before_last)
         after_inner()
         copy, at = edge_in(name, "outer", field, index)
 
@@ -405,16 +430,27 @@
 
         def high_inner():
             send_edge("h0", "inner", h, d)
-            deliver("high0", 0, high_piece(d), 2 * p_index + 1, d, start, d)
-
-        for dx in range(2):
-            @pl.when(d == dx)
-            def _(dx=dx):
-                arrive(1, dx)
-
-        field_network("e0", e, d, wa, 0, high, high_inner)
+
+            @pl.when(d == 1)
+            def _():
+                deliver("high0", 0, high_piece(d), 2 * p_index + 1, d, start, d)
+
+        def high_ready():
+            for dx in range(2):
+                @pl.when(d == dx)
+                def _(dx=dx):
+                    arrive(1, dx)
+                    if dx:
+                        for half in range(2):
+                            deliver("high0", half, high_piece(0), 2 * x + 1, 0, start, 0)
+
+        field_network("e0", e, d, wa, 0, high, high_inner, high_ready)
         send_edge("h0", "outer", h, d)
-        deliver("high0", 1, high_piece(d), 2 * p_index + 1, d, start, d)
+
+        @pl.when(d == 1)
+        def _():
+            deliver("high0", 1, high_piece(d), 2 * p_index + 1, d, start, d)
+
 
         def low(j, value):
             old = pair_of([e[1, d, edge + j], e[1, d, edge + j + 1]])
@@ -510,6 +546,7 @@
     layers = predict_w.shape[1]
     block = width // 4
     span = block + LANES
+    packed = rows * 8 * layers // LANES
     tiles = lax.axis_size("tile")
     vmem = pl.BlockSpec(memory_space=pltpu.VMEM)
     hbm = pl.BlockSpec(memory_space=pl.ANY)
@@ -530,7 +567,7 @@
             buffer(3, 2 * rows - 2), buffer(3, 2 * rows - 4), buffer(3, 2 * rows - 6),
             acc, acc, weight, weight, weight, weight,
             pltpu.VMEM((4 * layers, 2 * channels, LANES), jnp.float32),
-            buffer(3, rows, columns=2 * LANES), buffer(4, rows, columns=LANES),
+            buffer(3, rows, columns=2 * LANES), buffer(4, packed, columns=LANES), buffer(2, 2, packed, columns=LANES),
             pltpu.SemaphoreType.DMA((len(SEND),)),
             pltpu.SemaphoreType.DMA((len(RECV),)),
             pltpu.SemaphoreType.DMA((7,)),

time: 101 us -> 83.9 us (0.83)
  Pallas kernels: 92.4 us -> 74.4 us
    pallas_call x1, Pallas kernels: 92.4 us -> 74.4 us  [local(): pl.pallas_call(functools.partial(kernel, tiles), out_shape=jax.ShapeDtype...]
where the time goes in v2:
time: 83.9 us; the launch traced here: 82.5 us
  Pallas kernels  74.4 us (89%)
  local copies, waits for them, and re-layouts  8.12 us (10%)
    pallas_call x1, Pallas kernels, local(): pl.pallas_call(functools.partial(kernel, tiles), out_shape=jax.ShapeDtype...  74.4 us
    broadcast_in_dim x1, local copies, waits for them, and re-layouts, local(): return jnp.transpose(result, (1, 0, 2))[None]  4.06 us
    unnamed x1, local copies, waits for them, and re-layouts  4.06 us

profile of v2, /device:TPU:16, one launch (start us, length us, event | category | flops | bytes accessed | tf_op | source)
XLA Modules:
  0.0 82.5 jit_solution(3753905558904965112)
XLA Ops:
  0.0 4.1 %copy.9 = bf16[1,64,8,2048]{3,1,2,0:T(8,128)(2,1)} copy(bf16[1,64,8,2048]{3,2,1,0:T(8,128)(2,1)} %param.5) | data formatting | bytes 4194304 | tf_op args[0]
  4.1 74.4 %shard_map.55 = bf16[8,64,2048]{2,1,0:T(8,128)(2,1)} custom-call(bf16[8,64,2048]{2,1,0:T(8,128)(2,1)} %bitcast.9, bf16[2,4,3,3,64,64]{5,4,3,2,1,0:T(8,128)(2,1)} %pw.1, bf16[2,4,3,3,64,64]{5,4,3,2,1,0:T(8,128)(2,1)} %uw.1, f32[2,4,64]{2,1,0:T(4,128)} %pb.1, f32[2,4,64]{2,1,0:T(4,128)} %ub.1), custom_call_target="tpu_custom_call" | custom-call | tf_op jit(solution)/shard_map/pallas_call | solution.py:559
  78.5 4.1 %copy.7 = bf16[1,64,8,2048]{3,2,1,0:T(8,128)(2,1)} copy(bf16[1,64,8,2048]{3,1,2,0:T(8,128)(2,1)} %bitcast.8) | data formatting | bytes 4194304 | tf_op jit(solution)/shard_map/broadcast_in_dim | solution.py:579

commit v3 on v2

--- a/solution.py
+++ b/solution.py
@@ -36,7 +36,7 @@
     return v + d - 2 * v * d
 
 
-def kernel(tiles, own, pw, uw, pb, ub, out, e, o, h, fb, g2, l2, a_ref, c_ref, d_ref, acc0, acc1, wa, wb, wc, wd,
+def kernel(tiles, own, pw_in, uw_in, pb, ub, out, pw, uw, e, o, h, fb, g2, l2, a_ref, c_ref, d_ref, acc0, acc1, wa, wb, wc, wd,
            bias, cuts, pads, packs, send_sem, recv_sem, local_sem):
     rows, channels, width = own.shape
     layers = pw.shape[1]
@@ -89,19 +89,11 @@
         )
         for k in range(3)
     ]
-    for copy in cut_copies:
+    weight_copies = [
+        pltpu.make_async_copy(src, dst, local_sem.at[7 + k]) for k, (src, dst) in enumerate(((pw_in, pw), (uw_in, uw)))
+    ]
+    for copy in cut_copies + weight_copies:
         copy.start()
-
-    @pl.when(jnp.logical_not(has_outer))
-    def _():
-        zero = jnp.zeros((edge, channels, span), jnp.bfloat16)
-        at = pl.ds(3 * edge * core, edge)
-        for v in range(3):
-            for d in range(2):
-                e[v, d, at] = zero
-                h[v, d, at] = zero
-            fb[0, v, at] = zero
-            g2[v, at] = zero
 
     pl.semaphore_wait(barrier, 7 + has_outer.astype(jnp.int32))
 
@@ -230,6 +222,19 @@
             bias[base + layer, :channels] = full
             bias[base + layer, channels:] = full
 
+    @pl.when(jnp.logical_not(has_outer))
+    def _():
+        zero = jnp.zeros((edge, channels, span), jnp.bfloat16)
+        at = pl.ds(3 * edge * core, edge)
+        for v in range(3):
+            for d in range(2):
+                e[v, d, at] = zero
+                h[v, d, at] = zero
+            fb[0, v, at] = zero
+            g2[v, at] = zero
+
+    for copy in weight_copies:
+        copy.wait()
     for k, (k_ref, b_ref, level, w_ref) in enumerate(
         ((pw, pb, 0, wa), (uw, ub, 0, wb), (pw, pb, 1, wc), (uw, ub, 1, wd))
     ):
@@ -417,13 +422,6 @@
     def pair_network(d, carry):
         p_index = flip(x, d)
 
-        @pl.when(d == 1)
-        def _():
-            arrive(0, 1)
-            send_edge("e0", "inner", e, d)
-            send_edge("e0", "outer", e, d)
-            turn(e, (d,), edge, rows)
-
         def high(j, value):
             old = pair_of([o[d, j], o[d, j + 1]])
             emit(h, (d,), edge + j, old - value)
@@ -464,6 +462,13 @@
             @pl.when(x == d)
             def _():
                 send_edge("f", "inner", fb.at[0])
+
+            @pl.when(d == 0)
+            def _():
+                arrive(0, 1)
+                send_edge("e0", "inner", e, 1)
+                send_edge("e0", "outer", e, 1)
+                turn(e, (1,), edge, rows)
 
         field_network("h0", h, d, wb, layers, low, low_inner)
 
@@ -559,9 +564,10 @@
     result = pl.pallas_call(
         functools.partial(kernel, tiles),
         out_shape=jax.ShapeDtypeStruct(own.shape, jnp.bfloat16),
-        in_specs=[hbm, vmem, vmem, vmem, vmem],
+        in_specs=[hbm, hbm, hbm, vmem, vmem],
         out_specs=hbm,
         scratch_shapes=[
+            pltpu.VMEM(predict_w.shape, predict_w.dtype), pltpu.VMEM(update_w.shape, update_w.dtype),
             buffer(3, 2, 2 * rows), buffer(2, rows), buffer(3, 2, 2 * rows), buffer(2, 3, 2 * rows),
             buffer(3, 2 * rows), buffer(rows, columns=block),
             buffer(3, 2 * rows - 2), buffer(3, 2 * rows - 4), buffer(3, 2 * rows - 6),
@@ -570,7 +576,7 @@
             buffer(3, rows, columns=2 * LANES), buffer(4, packed, columns=LANES), buffer(2, 2, packed, columns=LANES),
             pltpu.SemaphoreType.DMA((len(SEND),)),
             pltpu.SemaphoreType.DMA((len(RECV),)),
-            pltpu.SemaphoreType.DMA((7,)),
+            pltpu.SemaphoreType.DMA((9,)),
         ],
         compiler_params=pltpu.CompilerParams(
             collective_id=0, has_side_effects=True, vmem_limit_bytes=60 * 1024 * 1024

time: 83.9 us -> 79.8 us (0.951); the launches traced: 82.5 us -> 79.5 us
  Pallas kernels: 74.4 us -> 71.4 us
    pallas_call x1, Pallas kernels: 74.4 us -> 71.4 us  [local(): pl.pallas_call(functools.partial(kernel, tiles), out_shape=jax.ShapeDtype...]
where the time goes in v3:
time: 79.8 us; the launch traced here: 79.5 us
  Pallas kernels  71.4 us (89%)
  local copies, waits for them, and re-layouts  8.12 us (10%)
    pallas_call x1, Pallas kernels, local(): pl.pallas_call(functools.partial(kernel, tiles), out_shape=jax.ShapeDtype...  71.4 us
    broadcast_in_dim x1, local copies, waits for them, and re-layouts, local(): return jnp.transpose(result, (1, 0, 2))[None]  4.06 us
    unnamed x1, local copies, waits for them, and re-layouts  4.06 us

profile of v3, /device:TPU:16, one launch (start us, length us, event | category | flops | bytes accessed | tf_op | source)
XLA Modules:
  0.0 79.5 jit_solution(10594148369972866639)
XLA Ops:
  0.0 4.1 %copy.9 = bf16[1,64,8,2048]{3,1,2,0:T(8,128)(2,1)} copy(bf16[1,64,8,2048]{3,2,1,0:T(8,128)(2,1)} %param.5) | data formatting | bytes 4194304 | tf_op args[0]
  4.1 71.4 %shard_map.55 = bf16[8,64,2048]{2,1,0:T(8,128)(2,1)} custom-call(bf16[8,64,2048]{2,1,0:T(8,128)(2,1)} %bitcast.9, bf16[2,4,3,3,64,64]{5,4,3,2,1,0:T(8,128)(2,1)} %pw_in.1, bf16[2,4,3,3,64,64]{5,4,3,2,1,0:T(8,128)(2,1)} %uw_in.1, f32[2,4,64]{2,1,0:T(4,128)} %pb.1, f32[2,4,64]{2,1,0:T(4,128)} %ub.1), custom_call_target="tpu_custom_call" | custom-call | tf_op jit(solution)/shard_map/pallas_call | solution.py:564
  75.5 4.1 %copy.7 = bf16[1,64,8,2048]{3,2,1,0:T(8,128)(2,1)} copy(bf16[1,64,8,2048]{3,1,2,0:T(8,128)(2,1)} %bitcast.8) | data formatting | bytes 4194304 | tf_op jit(solution)/shard_map/broadcast_in_dim | solution.py:585
